TPU v7x, 32 devices: a whole 2x2x4 slice. The times are simulated.
32 devices in a mesh: face: 4 (over x, core), tile: 8 (over z, y).
Axes of the slice: x: 2, y: 2, z: 4, core: 2. Of those that a mesh axis runs over, the one named last changes fastest.
Arguments:
- field_in: bfloat16 [12, 48, 256, 256], P('face', None, 'tile'), may hold values from -6 to 6
- out_grad: bfloat16 [12, 48, 256, 256], P('face', None, 'tile'), may hold values from -6 to 6
- weight_first: bfloat16 [48, 48, 3, 3], replicated, may hold values from -0.3125 to 0.3125
- bias_first: float32 [48], replicated, may hold values from -3 to 3
- weight_second: bfloat16 [48, 48, 3, 3], replicated, may hold values from -0.3125 to 0.3125
- bias_second: float32 [48], replicated, may hold values from -3 to 3
- face_links: int32 [12, 4, 3], replicated, may hold values from 0 to 11, as said below
- corner_rules: int32 [12, 4], replicated, may hold values from 0 to 1
Outputs:
- output_field: bfloat16 [12, 48, 256, 256], P('face', None, 'tile')
- grad_field: bfloat16 [12, 48, 256, 256], P('face', None, 'tile')
- grad_weight_first: float32 [48, 48, 3, 3], replicated
- grad_bias_first: float32 [48], replicated
- grad_weight_second: float32 [48, 48, 3, 3], replicated
- grad_bias_second: float32 [48], replicated
Inputs may be any that keep to these rules, and one draw needn't show every extreme that they name: face_links[f, e] = (g, e2, r) glues edge e of face f to edge e2 of face g; r = 1 when positions along the two edges run in opposite directions. The gluing is a pairing: (g, e2) differs from (f, e) and face_links[g, e2] = (f, e, r). The partner face lies in 0..11, the edge in 0..3, the flag in 0..1.
All inputs are finite; a program needn't handle non-finite values.
Results may differ from a plain program's by a relative error of at most 0.0055.
The roundings to bfloat16 on the way count: a program that leaves them out, or rounds other values in their place, can miss the bound.
Values may be sent and summed in bfloat16 or wider, within the bound.
A program may use at most 256 MiB of HBM per device.

v0:
```python
import jax
import jax.numpy as jnp
from jax import lax
from jax.sharding import PartitionSpec as P

INV_ROOT_TWO = 0.7071067811865476
INV_ROOT_TWO_PI = 0.3989422804014327


def shortened(x):
    return jax.tree.map(lambda a: a.astype(jnp.bfloat16) if a.dtype == jnp.float32 else a, x)


def extended_2(block, sides, width):
    for axis, dim in sides:
        count = lax.axis_size(axis)
        forward = [(i, i + 1) for i in range(count - 1)]
        backward = [(target, source) for source, target in forward]
        low = lax.ppermute(
            lax.slice_in_dim(block, block.shape[dim] - width, None, axis=dim), axis, forward
        )
        high = lax.ppermute(lax.slice_in_dim(block, 0, width, axis=dim), axis, backward)
        block = jnp.concatenate([low, block, high], axis=dim)
    return block


def gelu_pair(values):
    normal_cdf = 0.5 * (1.0 + lax.erf(values * INV_ROOT_TWO))
    normal_pdf = jnp.exp(-0.5 * values * values) * INV_ROOT_TWO_PI
    return (values * normal_cdf, normal_cdf + values * normal_pdf)


def convolve(padded, weight):
    return lax.conv_general_dilated(
        padded,
        weight,
        (1, 1),
        "VALID",
        dimension_numbers=("NCHW", "OIHW", "NCHW"),
        preferred_element_type=jnp.float32,
    )


def halo_rows(strip):
    return extended_2(shortened(strip), (("tile", 2),), 1).astype(strip.dtype)


def place_lines(north_row, south_row, west_part, east_part, tile_pos, tile_count):
    seg_len = west_part.shape[-1]
    mirrored = tile_count - 1 - tile_pos
    blanks = jnp.zeros(north_row.shape, jnp.float32)
    north_full = jnp.where(tile_pos == 0, north_row.astype(jnp.float32), blanks)
    south_full = jnp.where(tile_pos == tile_count - 1, south_row.astype(jnp.float32), blanks)
    west_wide = west_part.astype(jnp.float32)
    east_wide = east_part.astype(jnp.float32)
    west_full = lax.dynamic_update_slice_in_dim(blanks, west_wide, tile_pos * seg_len, 2)
    east_full = lax.dynamic_update_slice_in_dim(blanks, east_wide, tile_pos * seg_len, 2)
    placed = jnp.stack([north_full, south_full, west_full, east_full], axis=1)
    own_lines = lax.psum(placed.astype(jnp.bfloat16), "tile")
    front = lax.dynamic_slice_in_dim(own_lines, tile_pos * seg_len, seg_len, 3)
    back = lax.dynamic_slice_in_dim(own_lines, mirrored * seg_len, seg_len, 3)
    return (front, back)


def partner_pieces(front, my_links, tile_pos, tile_count):
    faces_dev, _, channels, seg_len = front.shape
    side_len = seg_len * tile_count
    partner_face = my_links[:, :, 0].reshape(-1)
    partner_edge = my_links[:, :, 1].reshape(-1)
    flip_mask = (my_links[:, :, 2] == 1).reshape(-1)
    gathered = lax.all_gather(front, ("face", "tile"), axis=3, tiled=True)

    def fetch_line(face_id, edge_id):
        start = (face_id % faces_dev, edge_id, 0, face_id // faces_dev * side_len)
        return lax.dynamic_slice(gathered, start, (1, 1, channels, side_len))[0, 0]

    source = jax.vmap(fetch_line)(partner_face, partner_edge)
    ghosts = jnp.where(flip_mask[:, None, None], source[:, :, ::-1], source)
    ghosts = ghosts.reshape(faces_dev, 4, channels, side_len)
    north_row = ghosts[:, 0]
    south_row = ghosts[:, 1]
    west_part = lax.dynamic_slice_in_dim(ghosts[:, 2], tile_pos * seg_len, seg_len, 2)
    east_part = lax.dynamic_slice_in_dim(ghosts[:, 3], tile_pos * seg_len, seg_len, 2)
    return (north_row, south_row, west_part, east_part)


def fill_strip(activation, my_links, my_corners, tile_pos, tile_count):
    front, back = place_lines(
        activation[:, :, 0, :],
        activation[:, :, -1, :],
        activation[:, :, :, 0],
        activation[:, :, :, -1],
        tile_pos,
        tile_count,
    )
    north_row, south_row, west_part, east_part = partner_pieces(
        front, my_links, tile_pos, tile_count
    )
    corner_code = (my_corners == 0)[:, :, None]
    corner_nw = jnp.where(corner_code[:, 0], north_row[:, :, 0], west_part[:, :, 0])
    corner_ne = jnp.where(corner_code[:, 1], north_row[:, :, -1], east_part[:, :, 0])
    corner_sw = jnp.where(corner_code[:, 2], south_row[:, :, 0], west_part[:, :, -1])
    corner_se = jnp.where(corner_code[:, 3], south_row[:, :, -1], east_part[:, :, -1])
    middle = jnp.concatenate(
        [west_part[:, :, :, None], activation, east_part[:, :, :, None]], axis=3
    )
    extended = halo_rows(middle)
    top_row = jnp.concatenate([corner_nw[:, :, None], north_row, corner_ne[:, :, None]], axis=2)
    bottom_row = jnp.concatenate([corner_sw[:, :, None], south_row, corner_se[:, :, None]], axis=2)
    top_rim = jnp.where(tile_pos == 0, top_row, extended[:, :, 0])
    bottom_rim = jnp.where(tile_pos == tile_count - 1, bottom_row, extended[:, :, -1])
    return jnp.concatenate(
        [top_rim[:, :, None], extended[:, :, 1:-1], bottom_rim[:, :, None]], axis=2
    )


def unfold_strip(cotangent, weight, my_links, my_corners, tile_pos, tile_count):
    widened = jnp.pad(cotangent, ((0, 0), (0, 0), (0, 0), (1, 1)))
    extended = halo_rows(widened)
    padded = jnp.pad(extended, ((0, 0), (0, 0), (1, 1), (1, 1)))
    flipped = jnp.transpose(weight[:, :, ::-1, ::-1], (1, 0, 2, 3))
    pad_grad = convolve(padded, flipped)
    at_top = tile_pos == 0
    at_bottom = tile_pos == tile_count - 1
    north_row = pad_grad[:, :, 0, 1:-1]
    south_row = pad_grad[:, :, -1, 1:-1]
    west_part = pad_grad[:, :, 1:-1, 0]
    east_part = pad_grad[:, :, 1:-1, -1]
    corner_nw = pad_grad[:, :, 0, 0]
    corner_ne = pad_grad[:, :, 0, -1]
    corner_sw = pad_grad[:, :, -1, 0]
    corner_se = pad_grad[:, :, -1, -1]
    corner_code = my_corners[:, :, None]
    north_row = north_row.at[:, :, 0].add(jnp.where(corner_code[:, 0] == 0, corner_nw, 0.0))
    north_row = north_row.at[:, :, -1].add(jnp.where(corner_code[:, 1] == 0, corner_ne, 0.0))
    south_row = south_row.at[:, :, 0].add(jnp.where(corner_code[:, 2] == 0, corner_sw, 0.0))
    south_row = south_row.at[:, :, -1].add(jnp.where(corner_code[:, 3] == 0, corner_se, 0.0))
    west_part = west_part.at[:, :, 0].add(
        jnp.where((corner_code[:, 0] == 1) & at_top, corner_nw, 0.0)
    )
    west_part = west_part.at[:, :, -1].add(
        jnp.where((corner_code[:, 2] == 1) & at_bottom, corner_sw, 0.0)
    )
    east_part = east_part.at[:, :, 0].add(
        jnp.where((corner_code[:, 1] == 1) & at_top, corner_ne, 0.0)
    )
    east_part = east_part.at[:, :, -1].add(
        jnp.where((corner_code[:, 3] == 1) & at_bottom, corner_se, 0.0)
    )
    front, back = place_lines(
        north_row.astype(jnp.bfloat16),
        south_row.astype(jnp.bfloat16),
        west_part.astype(jnp.bfloat16),
        east_part.astype(jnp.bfloat16),
        tile_pos,
        tile_count,
    )
    back_north, back_south, back_west, back_east = partner_pieces(
        front, my_links, tile_pos, tile_count
    )
    interior = pad_grad[:, :, 1:-1, 1:-1]
    interior = interior.at[:, :, 0, :].add(jnp.where(at_top, back_north.astype(jnp.float32), 0.0))
    interior = interior.at[:, :, -1, :].add(
        jnp.where(at_bottom, back_south.astype(jnp.float32), 0.0)
    )
    interior = interior.at[:, :, :, 0].add(back_west.astype(jnp.float32))
    interior = interior.at[:, :, :, -1].add(back_east.astype(jnp.float32))
    return interior


def weight_grad(cotangent, padded):
    return lax.conv_general_dilated(
        padded,
        cotangent,
        (1, 1),
        "VALID",
        dimension_numbers=("CNHW", "IOHW", "CNHW"),
        preferred_element_type=jnp.float32,
    )


def body(
    field_in,
    out_grad,
    weight_first,
    bias_first,
    weight_second,
    bias_second,
    face_links,
    corner_rules,
):
    tile_count = lax.axis_size("tile")
    tile_pos = lax.axis_index("tile")
    face_pos = lax.axis_index("face")
    faces_dev = field_in.shape[0]
    side_len = field_in.shape[3]
    my_links = lax.dynamic_slice_in_dim(face_links, face_pos * faces_dev, faces_dev, 0)
    my_corners = lax.dynamic_slice_in_dim(corner_rules, face_pos * faces_dev, faces_dev, 0)
    padded_first = fill_strip(field_in, my_links, my_corners, tile_pos, tile_count)
    pre_first = convolve(padded_first, weight_first) + bias_first[None, :, None, None]
    gelu_first, slope_first = gelu_pair(pre_first)
    hidden = gelu_first.astype(jnp.bfloat16)
    padded_second = fill_strip(hidden, my_links, my_corners, tile_pos, tile_count)
    pre_second = convolve(padded_second, weight_second) + bias_second[None, :, None, None]
    gelu_second, slope_second = gelu_pair(pre_second)
    output_field = gelu_second.astype(jnp.bfloat16)
    grad_second = (out_grad.astype(jnp.float32) * slope_second).astype(jnp.bfloat16)
    weight_second_part = weight_grad(grad_second, padded_second)
    bias_second_part = jnp.sum(grad_second.astype(jnp.float32), axis=(0, 2, 3))
    grad_hidden = unfold_strip(
        grad_second, weight_second, my_links, my_corners, tile_pos, tile_count
    )
    grad_first = (grad_hidden * slope_first).astype(jnp.bfloat16)
    weight_first_part = weight_grad(grad_first, padded_first)
    bias_first_part = jnp.sum(grad_first.astype(jnp.float32), axis=(0, 2, 3))
    grad_field = unfold_strip(
        grad_first, weight_first, my_links, my_corners, tile_pos, tile_count
    ).astype(jnp.bfloat16)
    totals = lax.psum(
        (weight_first_part, bias_first_part, weight_second_part, bias_second_part), ("face", "tile")
    )
    return (
        output_field,
        grad_field,
        totals[0] / side_len,
        totals[1] / side_len,
        totals[2] / side_len,
        totals[3] / side_len,
    )


def solution(mesh):
    return jax.shard_map(
        body,
        mesh=mesh,
        in_specs=(
            P("face", None, "tile", None),
            P("face", None, "tile", None),
            P(),
            P(),
            P(),
            P(),
            P(),
            P(),
        ),
        out_specs=(
            P("face", None, "tile", None),
            P("face", None, "tile", None),
            P(),
            P(),
            P(),
            P(),
        ),
        check_vma=False,
    )
```

profile of v0, /device:TPU:0, one launch (start us, length us, event | category | flops | bytes accessed | tf_op | source)
XLA Modules:
  0.0 1963.4 jit_solution(1567796698921269111)
XLA Ops:
  19.2 74.5 %all-reduce.10.cloned.1.call-done = bf16[3,4,48,256]{3,2,0,1:T(8,128)(2,1)} async-done(((bf16[3,4,48,256]{3,2,0,1:T(8,128)(2,1)}), bf16[3,4,48,256]{3,2,0,1:T(8,128)(2,1)}) %all-reduce.10.cloned.1.call-update) | async-done | bytes 294928 | tf_op jit(solution)/shard_map/psum | solution.py:59
  103.9 51.9 %all-gather.5.cloned.1.call-done = bf16[3,4,48,1024]{2,1,0,3:T(4,128)(2,1)} async-done(((bf16[3,4,48,32]{2,1,0,3:T(4,128)(2,1)}), bf16[3,4,48,1024]{2,1,0,3:T(4,128)(2,1)}) %all-gather.5.cloned.1.call-update) | async-done | bytes 1179664 | tf_op jit(solution)/shard_map/all_gather | solution.py:71
  179.5 17.8 fusion.87
  203.9 24.2 %copy.2867 = bf16[48,34,3,8,33]{4,3,0,2,1:T(8,128)(2,1)} copy(bf16[48,34,3,8,33]{0,2,4,3,1:T(4,128)(2,1)} %bitcast.324) | data formatting | bytes 5170176 | tf_op jit(solution)/shard_map/conv_general_dilated | solution.py:34
  268.8 23.4 %fusion.8 = (f32[32,24,33,48]{3,1,2,0:T(8,128)}, bf16[32,24,33,48]{3,1,2,0:T(8,128)(2,1)S(1)}) fusion(f32[48]{0:T(128)S(1)} %copy-done.49, pred[24,33]{0,1:T(8,128)(4,1)S(1)} %copy-done.53, bf16[48,48,3,3]{1,0,3,2:T(8,128)(2,1)S(1)} %copy-done.47, bf16[48,34,3,8,35]{0,3,2,4,1:T(8,128)(2,1)} %copy.2762), kind=kOutput, calls=%fused_computation.21 | convolution fusion | flops 1065664512 | bytes 10083288 | tf_op jit(solution)/shard_map/conv_general_dilated | solution.py:34
  311.7 72.1 %all-reduce.12.cloned.1.call-done = bf16[3,4,48,256]{3,2,0,1:T(8,128)(2,1)} async-done(((bf16[3,4,48,256]{3,2,0,1:T(8,128)(2,1)}), bf16[3,4,48,256]{3,2,0,1:T(8,128)(2,1)}) %all-reduce.12.cloned.1.call-update) | async-done | bytes 294928 | tf_op jit(solution)/shard_map/psum | solution.py:59
  386.0 59.4 %all-gather.7.cloned.1.call-done = bf16[3,4,48,1024]{2,1,0,3:T(4,128)(2,1)} async-done(((bf16[3,4,48,32]{2,1,0,3:T(4,128)(2,1)}), bf16[3,4,48,1024]{2,1,0,3:T(4,128)(2,1)}) %all-gather.7.cloned.1.call-update) | async-done | bytes 1179664 | tf_op jit(solution)/shard_map/all_gather | solution.py:71
  468.6 19.1 fusion.84
  494.3 24.2 %copy.2872 = bf16[48,34,3,8,33]{4,3,0,2,1:T(8,128)(2,1)} copy(bf16[48,34,3,8,33]{0,2,4,3,1:T(4,128)(2,1)} %bitcast.325) | data formatting | bytes 5170176 | tf_op jit(solution)/shard_map/conv_general_dilated | solution.py:34
  559.2 22.5 %fusion.12 = (f32[32,24,33,48]{3,1,2,0:T(8,128)}, bf16[32,24,33,48]{3,1,2,0:T(8,128)(2,1)}) fusion(f32[48]{0:T(128)S(1)} %copy-done.50, pred[24,33]{0,1:T(8,128)(4,1)S(1)} %copy-done.53, bf16[48,48,3,3]{1,0,3,2:T(8,128)(2,1)S(1)} %copy-done, bf16[48,34,3,8,35]{0,3,2,4,1:T(8,128)(2,1)} %copy.2782), kind=kOutput, calls=%fused_computation.25 | convolution fusion | flops 1065664512 | bytes 10083288 | tf_op jit(solution)/shard_map/conv_general_dilated | solution.py:34
  694.7 22.0 %convolution_select_fusion.1 = f32[34,24,33,48]{3,1,2,0:T(8,128)} fusion(bf16[48,48,3,3]{1,0,3,2:T(8,128)(2,1)S(1)} %copy-done, bf16[48,34,3,8,35]{0,3,2,4,1:T(8,128)(2,1)} %copy.2790, pred[24,33]{0,1:T(8,128)(4,1)S(1)} %copy-done.51), kind=kOutput, calls=%fused_computation.37 | convolution fusion | flops 1096153344 | bytes 7954200 | tf_op jit(solution)/shard_map/conv_general_dilated | solution.py:34
  746.0 17.6 copy.2888
  763.6 29.2 %fusion.67 = (f32[3,48,1,256]{2,1,0,3:T(8,128)}, f32[3,48,1,256]{2,1,0,3:T(8,128)}) fusion(f32[3,48,34,258]{2,1,0,3:T(8,128)} %bitcast.309), kind=kLoop, calls=%fused_computation.219 | loop fusion | bytes 589824 | tf_op jit(solution)/shard_map/slice | solution.py:125
  827.4 73.5 %all-reduce.14.cloned.1.call-done = bf16[3,4,48,256]{3,2,0,1:T(8,128)(2,1)} async-done(((bf16[3,4,48,256]{3,2,0,1:T(8,128)(2,1)}), bf16[3,4,48,256]{3,2,0,1:T(8,128)(2,1)}) %all-reduce.14.cloned.1.call-update) | async-done | bytes 294928 | tf_op jit(solution)/shard_map/psum | solution.py:59
  982.4 20.5 %slice_add_fusion.3 = f32[3,48,1,256]{2,1,0,3:T(8,128)} fusion(f32[3,48,1,256]{2,1,0,3:T(8,128)} %copy.2815, f32[3,48,34,258]{2,1,0,3:T(8,128)} %bitcast.315), kind=kLoop, calls=%fused_computation.14 | loop fusion | flops 36864 | bytes 442368 | tf_op jit(solution)/shard_map/add | solution.py:162
  1015.1 43.6 %scatter-add.94 = f32[3,48,32,256]{2,1,0,3:T(8,128)} dynamic-update-slice(f32[3,48,32,256]{2,1,0,3:T(8,128)} %slice.1002, f32[3,48,1,256]{2,1,0,3:T(8,128)} %slice_add_fusion.3, s32[]{:T(128)} %constant.616.clone.1, s32[]{:T(128)} %constant.616.clone.1, s32[]{:T(128)} %constant.616.clone.1, s32[]{:T(128)} %constant.616.clone.1) | dynamic-update-slice | bytes 294916 | tf_op jit(solution)/shard_map/scatter-add | solution.py:162
  1058.7 20.5 %slice_add_fusion.2 = f32[3,48,1,256]{2,1,0,3:T(8,128)} fusion(f32[3,48,1,256]{2,1,0,3:T(8,128)} %copy.2817, f32[3,48,32,256]{2,1,0,3:T(8,128)} %scatter-add.94), kind=kLoop, calls=%fused_computation.13 | loop fusion | flops 36864 | bytes 442368 | tf_op jit(solution)/shard_map/add | solution.py:163
  1079.2 73.5 %scatter-add.95 = f32[3,48,32,256]{2,1,0,3:T(8,128)} dynamic-update-slice(f32[3,48,32,256]{2,1,0,3:T(8,128)} %scatter-add.94, f32[3,48,1,256]{2,1,0,3:T(8,128)} %slice_add_fusion.2, s32[]{:T(128)} %constant.616.clone.1, s32[]{:T(128)} %constant.616.clone.1, s32[]{:T(128)} %constant.635.clone.1, s32[]{:T(128)} %constant.616.clone.1) | dynamic-update-slice | bytes 294916 | tf_op jit(solution)/shard_map/scatter-add | solution.py:163
  1207.4 44.8 %fusion.75 = f32[48,48,3,3]{0,1,3,2:T(8,128)} fusion(bf16[3,48,32,256]{1,0,3,2:T(4,128)(2,1)} %copy.2858, bf16[3,48,1,258]{1,0,3,2:T(4,128)(2,1)S(1)} %copy-done.15, bf16[3,48,32,1]{1,0,3,2:T(4,128)(2,1)S(1)} %copy-done.23, bf16[3,48,32,256]{1,0,3,2:T(4,128)(2,1)} %bitcast.319, bf16[3,48,32,1]{1,0,3,2:T(4,128)(2,1)S(1)} %copy-done.21, ...), kind=kOutput, calls=%fused_computation.227 | convolution fusion | flops 1031847552 | bytes 4968576 | tf_op jit(solution)/shard_map/conv_general_dilated | solution.py:172
  1342.3 21.8 %convolution_select_fusion = f32[34,24,33,48]{3,1,2,0:T(8,128)} fusion(bf16[48,48,3,3]{1,0,3,2:T(8,128)(2,1)S(1)} %copy-done.48, bf16[48,34,3,8,35]{0,3,2,4,1:T(8,128)(2,1)} %copy.2828, pred[24,33]{0,1:T(8,128)(4,1)S(1)} %copy-done.52), kind=kOutput, calls=%fused_computation.36 | convolution fusion | flops 1096153344 | bytes 7954200 | tf_op jit(solution)/shard_map/conv_general_dilated | solution.py:34
  1393.4 17.6 copy.2892
  1411.0 29.3 %fusion.66 = (f32[3,48,1,256]{2,1,0,3:T(8,128)}, f32[3,48,1,256]{2,1,0,3:T(8,128)}) fusion(f32[3,48,34,258]{2,1,0,3:T(8,128)} %bitcast.302), kind=kLoop, calls=%fused_computation.218 | loop fusion | bytes 589824 | tf_op jit(solution)/shard_map/slice | solution.py:125
  1475.0 44.8 %fusion.74 = f32[48,48,3,3]{0,1,3,2:T(8,128)} fusion(bf16[3,48,32,256]{1,0,3,2:T(4,128)(2,1)} %copy.2857, bf16[3,48,1,258]{1,0,3,2:T(4,128)(2,1)S(1)} %copy-done.11, bf16[3,48,32,1]{1,0,3,2:T(4,128)(2,1)S(1)} %copy-done.19, bf16[3,48,32,256]{1,0,3,2:T(4,128)(2,1)} %copy.2758, bf16[3,48,32,1]{1,0,3,2:T(4,128)(2,1)S(1)} %copy-done.17, ...), kind=kOutput, calls=%fused_computation.226 | convolution fusion | flops 1031847552 | bytes 4968576 | tf_op jit(solution)/shard_map/conv_general_dilated | solution.py:172
  1520.1 28.0 %all-reduce.16.cloned.1.call-done = bf16[3,4,48,256]{3,2,0,1:T(8,128)(2,1)} async-done(((bf16[3,4,48,256]{3,2,0,1:T(8,128)(2,1)}), bf16[3,4,48,256]{3,2,0,1:T(8,128)(2,1)}) %all-reduce.16.cloned.1.call-update) | async-done | bytes 294928 | tf_op jit(solution)/shard_map/psum | solution.py:59
  1567.8 39.3 %all-reduce.2 = (f32[48]{0:T(128)S(1)}, f32[48]{0:T(128)S(1)}) all-reduce(f32[48]{0:T(128)S(1)} %copy-done.46, f32[48]{0:T(128)S(1)} %copy-done.45), channel_id=1, replica_groups=mesh['face'=4,'tile'=8] {'face','tile'}, use_global_device_ids=true, to_apply=%region_6.7 | all-reduce | flops 96 | bytes 768 | tf_op jit(solution)/shard_map/psum | solution.py:219
  1608.2 16.6 slice.1030
  1624.8 54.6 %all-reduce.18.cloned.1.call-done = (f32[48,48,3,3]{0,1,3,2:T(8,128)}, f32[48,48,3,3]{0,1,3,2:T(8,128)}) async-done(((f32[48,48,3,3]{0,1,3,2:T(8,128)}, f32[48,48,3,3]{0,1,3,2:T(8,128)}), (f32[48,48,3,3]{0,1,3,2:T(8,128)}, f32[48,48,3,3]{0,1,3,2:T(8,128)})) %all-reduce.18.cloned.1.call-update) | async-done | bytes 165904 | tf_op jit(solution)/shard_map/psum | solution.py:219
  1683.0 60.5 %all-gather.11.cloned.1.call-done = bf16[3,4,48,1024]{2,1,0,3:T(4,128)(2,1)} async-done(((bf16[3,4,48,32]{2,1,0,3:T(4,128)(2,1)}), bf16[3,4,48,1024]{2,1,0,3:T(4,128)(2,1)}) %all-gather.11.cloned.1.call-update) | async-done | bytes 1179664 | tf_op jit(solution)/shard_map/all_gather | solution.py:71
  1760.5 20.5 %slice_add_fusion.1 = f32[3,48,1,256]{2,1,0,3:T(8,128)} fusion(f32[3,48,1,256]{2,1,0,3:T(8,128)} %copy.2852, f32[3,48,34,258]{2,1,0,3:T(8,128)} %bitcast.308), kind=kLoop, calls=%fused_computation.12 | loop fusion | flops 36864 | bytes 442368 | tf_op jit(solution)/shard_map/add | solution.py:162
  1793.2 43.6 %scatter-add.114 = f32[3,48,32,256]{2,1,0,3:T(8,128)} dynamic-update-slice(f32[3,48,32,256]{2,1,0,3:T(8,128)} %slice.1030, f32[3,48,1,256]{2,1,0,3:T(8,128)} %slice_add_fusion.1, s32[]{:T(128)} %constant.616.clone.1, s32[]{:T(128)} %constant.616.clone.1, s32[]{:T(128)} %constant.616.clone.1, s32[]{:T(128)} %constant.616.clone.1) | dynamic-update-slice | bytes 294916 | tf_op jit(solution)/shard_map/scatter-add | solution.py:162
  1836.8 20.5 %slice_add_fusion = f32[3,48,1,256]{2,1,0,3:T(8,128)} fusion(f32[3,48,1,256]{2,1,0,3:T(8,128)} %copy.2854, f32[3,48,32,256]{2,1,0,3:T(8,128)} %scatter-add.114), kind=kLoop, calls=%fused_computation.11 | loop fusion | flops 36864 | bytes 442368 | tf_op jit(solution)/shard_map/add | solution.py:163
  1857.3 73.6 %scatter-add.115 = f32[3,48,32,256]{2,1,0,3:T(8,128)} dynamic-update-slice(f32[3,48,32,256]{2,1,0,3:T(8,128)} %scatter-add.114, f32[3,48,1,256]{2,1,0,3:T(8,128)} %slice_add_fusion, s32[]{:T(128)} %constant.616.clone.1, s32[]{:T(128)} %constant.616.clone.1, s32[]{:T(128)} %constant.635.clone.1, s32[]{:T(128)} %constant.616.clone.1) | dynamic-update-slice | bytes 294916 | tf_op jit(solution)/shard_map/scatter-add | solution.py:163
  (365 shorter events, 742.7 us)
Async XLA Ops:
  7.2 552.0 %copy-start = (bf16[48,48,3,3]{1,0,3,2:T(8,128)(2,1)S(1)}, bf16[48,48,3,3]{1,0,3,2:T(8,128)(2,1)}, u32[]{:S(2)}) copy-start(bf16[48,48,3,3]{1,0,3,2:T(8,128)(2,1)} %param.60) | copy-start | bytes 124420
  7.2 86.5 %all-reduce.10.cloned.1.call-start = ((), (), s32[]{:S(2)}) async-start(), calls=%async_computation | async-start | bytes 589824 | tf_op jit(solution)/shard_map/psum | solution.py:59
  7.2 95.1 %copy-start.24 = (s32[12,4,3]{0,1,2:T(4,128)S(1)}, s32[12,4,3]{0,1,2:T(4,128)}, u32[]{:S(2)}) copy-start(s32[12,4,3]{0,1,2:T(4,128)} %param.62) | copy-start | bytes 1732
  7.3 96.2 %copy-start.44 = (s32[12,4]{0,1:T(4,128)S(1)}, s32[12,4]{0,1:T(4,128)}, u32[]{:S(2)}) copy-start(s32[12,4]{0,1:T(4,128)} %param.63) | copy-start | bytes 580
  19.2 136.6 %all-gather.5.cloned.1.call-start = ((), (), s32[]{:S(2)}) async-start(), calls=%async_computation.1 | async-start | bytes 3244032 | tf_op jit(solution)/shard_map/all_gather | solution.py:71
  95.5 288.3 %all-reduce.12.cloned.1.call-start = ((), (), s32[]{:S(2)}) async-start(), calls=%async_computation.2 | async-start | bytes 589824 | tf_op jit(solution)/shard_map/psum | solution.py:59
  103.4 345.7 %copy-start.25 = (pred[12]{0:T(512)(128)(4,1)}, pred[12]{0:T(512)(128)(4,1)S(1)}, u32[]{:S(2)}) copy-start(pred[12]{0:T(512)(128)(4,1)S(1)} %eq.133) | copy-start | bytes 40
  103.9 341.5 %copy-start.5 = (s32[12]{0:T(128)}, s32[12]{0:T(128)S(1)}, u32[]{:S(2)}) copy-start(s32[12]{0:T(128)S(1)} %fusion.63) | copy-start | bytes 148
  163.5 15.4 collective-permute-start
  167.1 12.0 collective-permute-start.1
  311.7 133.7 %all-gather.7.cloned.1.call-start = ((), (), s32[]{:S(2)}) async-start(), calls=%async_computation.3 | async-start | bytes 3244032 | tf_op jit(solution)/shard_map/all_gather | solution.py:71
  385.6 515.3 %all-reduce.14.cloned.1.call-start = ((), (), s32[]{:S(2)}) async-start(), calls=%async_computation.4 | async-start | bytes 589824 | tf_op jit(solution)/shard_map/psum | solution.py:59
  452.9 15.1 collective-permute-start.2
  456.3 12.0 collective-permute-start.3
  621.4 13.5 collective-permute-start.4
  625.8 9.1 collective-permute-start.5
  627.4 192.8 %copy-start.38 = (pred[3]{0:T(512)(128)(4,1)}, pred[3]{0:T(512)(128)(4,1)S(1)}, u32[]{:S(2)}) copy-start(pred[3]{0:T(512)(128)(4,1)S(1)} %get-tuple-element.458) | copy-start | bytes 13
  627.4 192.8 %copy-start.40 = (pred[3]{0:T(512)(128)(4,1)}, pred[3]{0:T(512)(128)(4,1)S(1)}, u32[]{:S(2)}) copy-start(pred[3]{0:T(512)(128)(4,1)S(1)} %get-tuple-element.462) | copy-start | bytes 13
  627.4 192.8 %copy-start.42 = (pred[3]{0:T(512)(128)(4,1)}, pred[3]{0:T(512)(128)(4,1)S(1)}, u32[]{:S(2)}) copy-start(pred[3]{0:T(512)(128)(4,1)S(1)} %get-tuple-element.463) | copy-start | bytes 13
  627.5 194.5 %copy-start.30 = (pred[3]{0:T(512)(128)(4,1)}, pred[3]{0:T(512)(128)(4,1)S(1)}, u32[]{:S(2)}) copy-start(pred[3]{0:T(512)(128)(4,1)S(1)} %get-tuple-element.456) | copy-start | bytes 13
  627.5 194.5 %copy-start.32 = (pred[3]{0:T(512)(128)(4,1)}, pred[3]{0:T(512)(128)(4,1)S(1)}, u32[]{:S(2)}) copy-start(pred[3]{0:T(512)(128)(4,1)S(1)} %get-tuple-element.457) | copy-start | bytes 13
  627.5 194.5 %copy-start.34 = (pred[3]{0:T(512)(128)(4,1)}, pred[3]{0:T(512)(128)(4,1)S(1)}, u32[]{:S(2)}) copy-start(pred[3]{0:T(512)(128)(4,1)S(1)} %get-tuple-element.460) | copy-start | bytes 13
  627.5 194.5 %copy-start.36 = (pred[3]{0:T(512)(128)(4,1)}, pred[3]{0:T(512)(128)(4,1)S(1)}, u32[]{:S(2)}) copy-start(pred[3]{0:T(512)(128)(4,1)S(1)} %get-tuple-element.461) | copy-start | bytes 13
  627.5 196.7 %copy-start.28 = (pred[3]{0:T(512)(128)(4,1)}, pred[3]{0:T(512)(128)(4,1)S(1)}, u32[]{:S(2)}) copy-start(pred[3]{0:T(512)(128)(4,1)S(1)} %get-tuple-element.459) | copy-start | bytes 13
  827.4 137.6 %all-gather.9.cloned.1.call-start = ((), (), s32[]{:S(2)}) async-start(), calls=%async_computation.5 | async-start | bytes 3244032 | tf_op jit(solution)/shard_map/all_gather | solution.py:71
  902.8 645.3 %all-reduce.16.cloned.1.call-start = ((), (), s32[]{:S(2)}) async-start(), calls=%async_computation.6 | async-start | bytes 589824 | tf_op jit(solution)/shard_map/psum | solution.py:59
  1191.2 90.2 %collective-permute-start.6 = (bf16[3,48,1,258]{3,1,2,0:T(8,128)(2,1)}, bf16[3,48,1,258]{3,1,2,0:T(8,128)(2,1)}, u32[]{:S(2)}, u32[]{:S(2)}) collective-permute-start(bf16[3,48,1,258]{3,1,2,0:T(8,128)(2,1)} %copy.2824), channel_id=1, source_target_pairs={{0,1},{1,2},{2,3},{3,4},{4,5},{5,6},{6,7},{8,9},{9,10},{10,11},{11... | collective-permute-start | bytes 222920 | tf_op jit(solution)/shard_map/ppermute | solution.py:19
  1206.1 75.3 %collective-permute-start.7 = (bf16[3,48,1,258]{3,1,2,0:T(8,128)(2,1)}, bf16[3,48,1,258]{3,1,2,0:T(8,128)(2,1)}, u32[]{:S(2)}, u32[]{:S(2)}) collective-permute-start(bf16[3,48,1,258]{3,1,2,0:T(8,128)(2,1)} %copy.2825), channel_id=1, source_target_pairs={{1,0},{2,1},{3,2},{4,3},{5,4},{6,5},{7,6},{9,8},{10,9},{11,10},{12... | collective-permute-start | bytes 222920 | tf_op jit(solution)/shard_map/ppermute | solution.py:22
  1474.9 204.5 %all-reduce.18.cloned.1.call-start = ((), (), s32[]{:S(2)}) async-start(), calls=%async_computation.8 | async-start | bytes 884736 | tf_op jit(solution)/shard_map/psum | solution.py:219
  1519.8 223.6 %all-gather.11.cloned.1.call-start = ((), (), s32[]{:S(2)}) async-start(), calls=%async_computation.7 | async-start | bytes 3244032 | tf_op jit(solution)/shard_map/all_gather | solution.py:71
  1608.2 135.2 %copy-start.7 = (s32[12]{0:T(128)S(1)}, s32[12]{0:T(128)}, u32[]{:S(2)}) copy-start(s32[12]{0:T(128)} %copy-done.5) | copy-start | bytes 148
  1608.2 139.0 %copy-start.27 = (pred[12]{0:T(512)(128)(4,1)S(1)}, pred[12]{0:T(512)(128)(4,1)}, u32[]{:S(2)}) copy-start(pred[12]{0:T(512)(128)(4,1)} %copy-done.25) | copy-start | bytes 40
  (39 other events, 895.6 us)
Sparse Core Ops, SparseCore 0:
  19.3 74.3 all-reduce.9
  97.6 58.1 all-gather.4
  311.8 71.9 all-reduce.11
  387.2 58.1 all-gather.6
  827.5 73.4 all-reduce.13
  904.7 58.1 all-gather.8
  1475.0 72.9 all-reduce.15
  1554.0 125.3 all-reduce.17
  1683.3 60.0 all-gather.10
where the time goes:
time: 1990 us; the launch traced here: 1960 us
  local copies, waits for them, and re-layouts  973 us (49%)
  waiting for transfers between devices  499 us (25%)
  other arithmetic  236 us (12%)
  matrix products  179 us (9%)
  blocking collectives  39.3 us (2%)
  starting transfers between devices  21.1 us (1%)
    psum x4, waiting for transfers between devices, place_lines(): own_lines = lax.psum(placed.astype(jnp.bfloat16), 'tile')  248 us
    conv_general_dilated x16, local copies, waits for them, and re-layouts, convolve(): lax.conv_general_dilated(padded, weight, (1, 1), 'VALID', dimension_numbe...  238 us
    all_gather x4, waiting for transfers between devices, partner_pieces(): gathered = lax.all_gather(front, ('face', 'tile'), axis=3, tiled=True)  172 us
    scatter-add x2, local copies, waits for them, and re-layouts, unfold_strip(): interior.at[:, :, -1, :]  147 us
    unnamed x128, local copies, waits for them, and re-layouts  125 us
    conv_general_dilated x4, matrix products, convolve(): lax.conv_general_dilated(padded, weight, (1, 1), 'VALID', dimension_numbe...  89.7 us
    conv_general_dilated x2, matrix products, weight_grad(): lax.conv_general_dilated(padded, cotangent, (1, 1), 'VALID', dimension_nu...  89.7 us
    scatter-add x2, local copies, waits for them, and re-layouts, unfold_strip(): interior.at[:, :, 0, :]  87.2 us
  transfers between devices with their start and end apart: 17, of which 11 were waited for; matrix products, arithmetic and copies ran while one was open for 13% of the time, Pallas kernels for 0%

commit v1 on v0

--- a/solution.py
+++ b/solution.py
@@ -217,7 +217,10 @@
         grad_first, weight_first, my_links, my_corners, tile_pos, tile_count
     ).astype(jnp.bfloat16)
     totals = lax.psum(
-        (weight_first_part, bias_first_part, weight_second_part, bias_second_part), ("face", "tile")
+        lax.psum(
+            (weight_first_part, bias_first_part, weight_second_part, bias_second_part), "tile"
+        ),
+        "face",
     )
     return (
         output_field,

time: 1990 us -> 1900 us (0.955)
  waiting for transfers between devices: 499 us -> 415 us
    psum x1, waiting for transfers between devices: 54.6 us -> 0.02 us  [body(): lax.psum((weight_first_part, bias_first_part, weight_second_part, bias_se...]
    all_gather x4, waiting for transfers between devices: 172 us -> 143 us  [partner_pieces(): gathered = lax.all_gather(front, ('face', 'tile'), axis=3, tiled=True)]
    unnamed x128 -> x126, local copies, waits for them, and re-layouts: 125 us -> 125 us
  transfers between devices with their start and end apart: 17 -> 18, of which waited for: 11 -> 10; matrix products, arithmetic and copies ran while one was open for 13% -> 23% of each run, Pallas kernels for 0% -> 0%
where the time goes in v1:
time: 1900 us; the launch traced here: 1880 us
  local copies, waits for them, and re-layouts  979 us (52%)
  waiting for transfers between devices  415 us (22%)
  other arithmetic  240 us (13%)
  matrix products  180 us (9%)
  blocking collectives  25.3 us (1%)
  starting transfers between devices  21.2 us (1%)
    psum x4, waiting for transfers between devices, place_lines(): own_lines = lax.psum(placed.astype(jnp.bfloat16), 'tile')  247 us
    conv_general_dilated x16, local copies, waits for them, and re-layouts, convolve(): lax.conv_general_dilated(padded, weight, (1, 1), 'VALID', dimension_numbe...  238 us
    scatter-add x2, local copies, waits for them, and re-layouts, unfold_strip(): interior.at[:, :, -1, :]  147 us
    all_gather x4, waiting for transfers between devices, partner_pieces(): gathered = lax.all_gather(front, ('face', 'tile'), axis=3, tiled=True)  143 us
    unnamed x126, local copies, waits for them, and re-layouts  125 us
    conv_general_dilated x4, matrix products, convolve(): lax.conv_general_dilated(padded, weight, (1, 1), 'VALID', dimension_numbe...  90 us
    conv_general_dilated x2, matrix products, weight_grad(): lax.conv_general_dilated(padded, cotangent, (1, 1), 'VALID', dimension_nu...  89.8 us
    scatter-add x2, local copies, waits for them, and re-layouts, unfold_strip(): interior.at[:, :, 0, :]  87.2 us
  transfers between devices with their start and end apart: 18, of which 10 were waited for; matrix products, arithmetic and copies ran while one was open for 23% of the time, Pallas kernels for 0%

profile of v1, /device:TPU:0, one launch (start us, length us, event | category | flops | bytes accessed | tf_op | source)
XLA Modules:
  0.0 1876.3 jit_solution(5511332149891210849)
XLA Ops:
  19.2 74.5 %all-reduce.13.cloned.1.call-done = bf16[3,4,48,256]{3,2,0,1:T(8,128)(2,1)} async-done(((bf16[3,4,48,256]{3,2,0,1:T(8,128)(2,1)}), bf16[3,4,48,256]{3,2,0,1:T(8,128)(2,1)}) %all-reduce.13.cloned.1.call-update) | async-done | bytes 294928 | tf_op jit(solution)/shard_map/psum | solution.py:59
  103.9 51.9 %all-gather.5.cloned.1.call-done = bf16[3,4,48,1024]{2,1,0,3:T(4,128)(2,1)} async-done(((bf16[3,4,48,32]{2,1,0,3:T(4,128)(2,1)}), bf16[3,4,48,1024]{2,1,0,3:T(4,128)(2,1)}) %all-gather.5.cloned.1.call-update) | async-done | bytes 1179664 | tf_op jit(solution)/shard_map/all_gather | solution.py:71
  179.4 17.8 fusion.87
  203.9 24.2 %copy.2867 = bf16[48,34,3,8,33]{4,3,0,2,1:T(8,128)(2,1)} copy(bf16[48,34,3,8,33]{0,2,4,3,1:T(4,128)(2,1)} %bitcast.324) | data formatting | bytes 5170176 | tf_op jit(solution)/shard_map/conv_general_dilated | solution.py:34
  268.6 23.4 %fusion.8 = (f32[32,24,33,48]{3,1,2,0:T(8,128)}, bf16[32,24,33,48]{3,1,2,0:T(8,128)(2,1)S(1)}) fusion(f32[48]{0:T(128)S(1)} %copy-done.48, pred[24,33]{0,1:T(8,128)(4,1)S(1)} %copy-done.52, bf16[48,48,3,3]{1,0,3,2:T(8,128)(2,1)S(1)} %copy-done.46, bf16[48,34,3,8,35]{0,3,2,4,1:T(8,128)(2,1)} %copy.2762), kind=kOutput, calls=%fused_computation.21 | convolution fusion | flops 1065664512 | bytes 10083288 | tf_op jit(solution)/shard_map/conv_general_dilated | solution.py:34
  311.4 72.2 %all-reduce.15.cloned.1.call-done = bf16[3,4,48,256]{3,2,0,1:T(8,128)(2,1)} async-done(((bf16[3,4,48,256]{3,2,0,1:T(8,128)(2,1)}), bf16[3,4,48,256]{3,2,0,1:T(8,128)(2,1)}) %all-reduce.15.cloned.1.call-update) | async-done | bytes 294928 | tf_op jit(solution)/shard_map/psum | solution.py:59
  385.8 59.4 %all-gather.7.cloned.1.call-done = bf16[3,4,48,1024]{2,1,0,3:T(4,128)(2,1)} async-done(((bf16[3,4,48,32]{2,1,0,3:T(4,128)(2,1)}), bf16[3,4,48,1024]{2,1,0,3:T(4,128)(2,1)}) %all-gather.7.cloned.1.call-update) | async-done | bytes 1179664 | tf_op jit(solution)/shard_map/all_gather | solution.py:71
  468.3 19.1 %fusion.84 = bf16[48,34,3,258]{0,2,3,1:T(4,128)(2,1)S(1)} fusion(bf16[3,48,1,258]{1,0,3,2:T(4,128)(2,1)S(1)} %maximum_select_fusion.3, bf16[3,48,32,1]{1,0,3,2:T(4,128)(2,1)S(1)} %copy.2779, bf16[3,48,32,256]{1,0,3,2:T(4,128)(2,1)} %bitcast.318, bf16[3,48,32,1]{1,0,3,2:T(4,128)(2,1)S(1)} %copy.2778, bf16[3,48,1,258]{1,0,3,2:T(4,128)(2,1)S(1)} %maximum_select_fusion.2), kind=kLoop, calls=%fused_computation.228 | loop fusion | flops 5052672 | bytes 5052672 | tf_op jit(solution)/shard_map/concatenate | solution.py:112
  494.1 24.2 %copy.2872 = bf16[48,34,3,8,33]{4,3,0,2,1:T(8,128)(2,1)} copy(bf16[48,34,3,8,33]{0,2,4,3,1:T(4,128)(2,1)} %bitcast.325) | data formatting | bytes 5170176 | tf_op jit(solution)/shard_map/conv_general_dilated | solution.py:34
  558.8 22.5 %fusion.12 = (f32[32,24,33,48]{3,1,2,0:T(8,128)}, bf16[32,24,33,48]{3,1,2,0:T(8,128)(2,1)}) fusion(f32[48]{0:T(128)S(1)} %copy-done.49, pred[24,33]{0,1:T(8,128)(4,1)S(1)} %copy-done.52, bf16[48,48,3,3]{1,0,3,2:T(8,128)(2,1)S(1)} %copy-done, bf16[48,34,3,8,35]{0,3,2,4,1:T(8,128)(2,1)} %copy.2782), kind=kOutput, calls=%fused_computation.25 | convolution fusion | flops 1065664512 | bytes 10083288 | tf_op jit(solution)/shard_map/conv_general_dilated | solution.py:34
  694.0 22.1 %convolution_select_fusion.1 = f32[34,24,33,48]{3,1,2,0:T(8,128)} fusion(bf16[48,48,3,3]{1,0,3,2:T(8,128)(2,1)S(1)} %copy-done, bf16[48,34,3,8,35]{0,3,2,4,1:T(8,128)(2,1)} %copy.2790, pred[24,33]{0,1:T(8,128)(4,1)S(1)} %copy-done.50), kind=kOutput, calls=%fused_computation.37 | convolution fusion | flops 1096153344 | bytes 7954200 | tf_op jit(solution)/shard_map/conv_general_dilated | solution.py:34
  745.4 17.6 copy.2888
  763.1 28.9 %fusion.67 = (f32[3,48,1,256]{2,1,0,3:T(8,128)}, f32[3,48,1,256]{2,1,0,3:T(8,128)}) fusion(f32[3,48,34,258]{2,1,0,3:T(8,128)} %bitcast.309), kind=kLoop, calls=%fused_computation.219 | loop fusion | bytes 589824 | tf_op jit(solution)/shard_map/slice | solution.py:125
  872.2 28.1 %all-reduce.17.cloned.1.call-done = bf16[3,4,48,256]{3,2,0,1:T(8,128)(2,1)} async-done(((bf16[3,4,48,256]{3,2,0,1:T(8,128)(2,1)}), bf16[3,4,48,256]{3,2,0,1:T(8,128)(2,1)}) %all-reduce.17.cloned.1.call-update) | async-done | bytes 294928 | tf_op jit(solution)/shard_map/psum | solution.py:59
  902.1 45.0 %fusion.75 = f32[48,48,3,3]{0,1,3,2:T(8,128)} fusion(bf16[3,48,32,256]{1,0,3,2:T(4,128)(2,1)} %copy.2858, bf16[3,48,1,258]{1,0,3,2:T(4,128)(2,1)S(1)} %copy-done.14, bf16[3,48,32,1]{1,0,3,2:T(4,128)(2,1)S(1)} %copy-done.22, bf16[3,48,32,256]{1,0,3,2:T(4,128)(2,1)} %bitcast.319, bf16[3,48,32,1]{1,0,3,2:T(4,128)(2,1)S(1)} %copy-done.20, ...), kind=kOutput, calls=%fused_computation.227 | convolution fusion | flops 1031847552 | bytes 4968576 | tf_op jit(solution)/shard_map/conv_general_dilated | solution.py:172
  981.2 20.5 %slice_add_fusion.3 = f32[3,48,1,256]{2,1,0,3:T(8,128)} fusion(f32[3,48,1,256]{2,1,0,3:T(8,128)} %copy.2815, f32[3,48,34,258]{2,1,0,3:T(8,128)} %bitcast.315), kind=kLoop, calls=%fused_computation.14 | loop fusion | flops 36864 | bytes 442368 | tf_op jit(solution)/shard_map/add | solution.py:162
  1013.9 43.6 %scatter-add.94 = f32[3,48,32,256]{2,1,0,3:T(8,128)} dynamic-update-slice(f32[3,48,32,256]{2,1,0,3:T(8,128)} %slice.1002, f32[3,48,1,256]{2,1,0,3:T(8,128)} %slice_add_fusion.3, s32[]{:T(128)} %constant.616.clone.1, s32[]{:T(128)} %constant.616.clone.1, s32[]{:T(128)} %constant.616.clone.1, s32[]{:T(128)} %constant.616.clone.1) | dynamic-update-slice | bytes 294916 | tf_op jit(solution)/shard_map/scatter-add | solution.py:162
  1057.6 20.9 %slice_add_fusion.2 = f32[3,48,1,256]{2,1,0,3:T(8,128)} fusion(f32[3,48,1,256]{2,1,0,3:T(8,128)} %copy.2817, f32[3,48,32,256]{2,1,0,3:T(8,128)} %scatter-add.94), kind=kLoop, calls=%fused_computation.13 | loop fusion | flops 36864 | bytes 442368 | tf_op jit(solution)/shard_map/add | solution.py:163
  1078.5 73.6 %scatter-add.95 = f32[3,48,32,256]{2,1,0,3:T(8,128)} dynamic-update-slice(f32[3,48,32,256]{2,1,0,3:T(8,128)} %scatter-add.94, f32[3,48,1,256]{2,1,0,3:T(8,128)} %slice_add_fusion.2, s32[]{:T(128)} %constant.616.clone.1, s32[]{:T(128)} %constant.616.clone.1, s32[]{:T(128)} %constant.635.clone.1, s32[]{:T(128)} %constant.616.clone.1) | dynamic-update-slice | bytes 294916 | tf_op jit(solution)/shard_map/scatter-add | solution.py:163
  1155.2 17.1 convert_reduce_fusion
  1187.3 17.4 pad_slice_fusion.3
  1232.8 44.8 %fusion.74 = f32[48,48,3,3]{0,1,3,2:T(8,128)} fusion(bf16[3,48,32,256]{1,0,3,2:T(4,128)(2,1)} %copy.2857, bf16[3,48,1,258]{1,0,3,2:T(4,128)(2,1)S(1)} %copy-done.10, bf16[3,48,32,1]{1,0,3,2:T(4,128)(2,1)S(1)} %copy-done.18, bf16[3,48,32,256]{1,0,3,2:T(4,128)(2,1)} %copy.2758, bf16[3,48,32,1]{1,0,3,2:T(4,128)(2,1)S(1)} %copy-done.16, ...), kind=kOutput, calls=%fused_computation.226 | convolution fusion | flops 1031847552 | bytes 4968576 | tf_op jit(solution)/shard_map/conv_general_dilated | solution.py:172
  1352.8 21.9 %convolution_select_fusion = f32[34,24,33,48]{3,1,2,0:T(8,128)} fusion(bf16[48,48,3,3]{1,0,3,2:T(8,128)(2,1)S(1)} %copy-done.47, bf16[48,34,3,8,35]{0,3,2,4,1:T(8,128)(2,1)} %copy.2828, pred[24,33]{0,1:T(8,128)(4,1)S(1)} %copy-done.51), kind=kOutput, calls=%fused_computation.36 | convolution fusion | flops 1096153344 | bytes 7954200 | tf_op jit(solution)/shard_map/conv_general_dilated | solution.py:34
  1404.0 17.6 copy.2892
  1421.6 29.0 %fusion.66 = (f32[3,48,1,256]{2,1,0,3:T(8,128)}, f32[3,48,1,256]{2,1,0,3:T(8,128)}) fusion(f32[3,48,34,258]{2,1,0,3:T(8,128)} %bitcast.302), kind=kLoop, calls=%fused_computation.218 | loop fusion | bytes 589824 | tf_op jit(solution)/shard_map/slice | solution.py:125
  1486.0 72.4 %all-reduce.19.cloned.1.call-done = bf16[3,4,48,256]{3,2,0,1:T(8,128)(2,1)} async-done(((bf16[3,4,48,256]{3,2,0,1:T(8,128)(2,1)}), bf16[3,4,48,256]{3,2,0,1:T(8,128)(2,1)}) %all-reduce.19.cloned.1.call-update) | async-done | bytes 294928 | tf_op jit(solution)/shard_map/psum | solution.py:59
  1578.1 19.5 %all-reduce.2 = (f32[48]{0:T(128)S(1)}, f32[48]{0:T(128)S(1)}) all-reduce(f32[48]{0:T(128)S(1)} %copy-done.45, f32[48]{0:T(128)S(1)} %copy-done.44), channel_id=1, replica_groups=mesh['face'=4,'tile'=8] {'tile'}, use_global_device_ids=true, to_apply=%region_7.8 | all-reduce | flops 96 | bytes 768 | tf_op jit(solution)/shard_map/psum | solution.py:220
  1624.5 31.2 %all-gather.11.cloned.1.call-done = bf16[3,4,48,1024]{2,1,0,3:T(4,128)(2,1)} async-done(((bf16[3,4,48,32]{2,1,0,3:T(4,128)(2,1)}), bf16[3,4,48,1024]{2,1,0,3:T(4,128)(2,1)}) %all-gather.11.cloned.1.call-update) | async-done | bytes 1179664 | tf_op jit(solution)/shard_map/all_gather | solution.py:71
  1673.1 20.6 %slice_add_fusion.1 = f32[3,48,1,256]{2,1,0,3:T(8,128)} fusion(f32[3,48,1,256]{2,1,0,3:T(8,128)} %copy.2852, f32[3,48,34,258]{2,1,0,3:T(8,128)} %bitcast.308), kind=kLoop, calls=%fused_computation.12 | loop fusion | flops 36864 | bytes 442368 | tf_op jit(solution)/shard_map/add | solution.py:162
  1705.8 43.6 %scatter-add.114 = f32[3,48,32,256]{2,1,0,3:T(8,128)} dynamic-update-slice(f32[3,48,32,256]{2,1,0,3:T(8,128)} %slice.1030, f32[3,48,1,256]{2,1,0,3:T(8,128)} %slice_add_fusion.1, s32[]{:T(128)} %constant.616.clone.1, s32[]{:T(128)} %constant.616.clone.1, s32[]{:T(128)} %constant.616.clone.1, s32[]{:T(128)} %constant.616.clone.1) | dynamic-update-slice | bytes 294916 | tf_op jit(solution)/shard_map/scatter-add | solution.py:162
  1749.4 20.5 %slice_add_fusion = f32[3,48,1,256]{2,1,0,3:T(8,128)} fusion(f32[3,48,1,256]{2,1,0,3:T(8,128)} %copy.2854, f32[3,48,32,256]{2,1,0,3:T(8,128)} %scatter-add.114), kind=kLoop, calls=%fused_computation.11 | loop fusion | flops 36864 | bytes 442368 | tf_op jit(solution)/shard_map/add | solution.py:163
  1769.9 73.6 %scatter-add.115 = f32[3,48,32,256]{2,1,0,3:T(8,128)} dynamic-update-slice(f32[3,48,32,256]{2,1,0,3:T(8,128)} %scatter-add.114, f32[3,48,1,256]{2,1,0,3:T(8,128)} %slice_add_fusion, s32[]{:T(128)} %constant.616.clone.1, s32[]{:T(128)} %constant.616.clone.1, s32[]{:T(128)} %constant.635.clone.1, s32[]{:T(128)} %constant.616.clone.1) | dynamic-update-slice | bytes 294916 | tf_op jit(solution)/shard_map/scatter-add | solution.py:163
  (367 shorter events, 741.7 us)
Async XLA Ops:
  7.2 551.7 %copy-start = (bf16[48,48,3,3]{1,0,3,2:T(8,128)(2,1)S(1)}, bf16[48,48,3,3]{1,0,3,2:T(8,128)(2,1)}, u32[]{:S(2)}) copy-start(bf16[48,48,3,3]{1,0,3,2:T(8,128)(2,1)} %param.60) | copy-start | bytes 124420
  7.2 88.4 %copy-start.3 = (bf16[3,48,32,256]{3,2,1,0:T(8,128)(2,1)S(1)}, bf16[3,48,32,256]{3,2,1,0:T(8,128)(2,1)}, u32[]{:S(2)}) copy-start(bf16[3,48,32,256]{3,2,1,0:T(8,128)(2,1)} %param.56) | copy-start | bytes 7077892
  7.2 86.5 %all-reduce.13.cloned.1.call-start = ((), (), s32[]{:S(2)}) async-start(), calls=%async_computation | async-start | bytes 589824 | tf_op jit(solution)/shard_map/psum | solution.py:59
  7.2 95.1 %copy-start.23 = (s32[12,4,3]{0,1,2:T(4,128)S(1)}, s32[12,4,3]{0,1,2:T(4,128)}, u32[]{:S(2)}) copy-start(s32[12,4,3]{0,1,2:T(4,128)} %param.62) | copy-start | bytes 1732
  7.3 96.2 %copy-start.43 = (s32[12,4]{0,1:T(4,128)S(1)}, s32[12,4]{0,1:T(4,128)}, u32[]{:S(2)}) copy-start(s32[12,4]{0,1:T(4,128)} %param.63) | copy-start | bytes 580
  19.2 136.7 %all-gather.5.cloned.1.call-start = ((), (), s32[]{:S(2)}) async-start(), calls=%async_computation.1 | async-start | bytes 3244032 | tf_op jit(solution)/shard_map/all_gather | solution.py:71
  95.5 288.1 %all-reduce.15.cloned.1.call-start = ((), (), s32[]{:S(2)}) async-start(), calls=%async_computation.2 | async-start | bytes 589824 | tf_op jit(solution)/shard_map/psum | solution.py:59
  103.4 345.6 %copy-start.24 = (pred[12]{0:T(512)(128)(4,1)}, pred[12]{0:T(512)(128)(4,1)S(1)}, u32[]{:S(2)}) copy-start(pred[12]{0:T(512)(128)(4,1)S(1)} %eq.133) | copy-start | bytes 40
  103.9 341.3 %copy-start.4 = (s32[12]{0:T(128)}, s32[12]{0:T(128)S(1)}, u32[]{:S(2)}) copy-start(s32[12]{0:T(128)S(1)} %fusion.63) | copy-start | bytes 148
  163.6 15.3 collective-permute-start
  167.2 11.9 collective-permute-start.1
  311.4 133.8 %all-gather.7.cloned.1.call-start = ((), (), s32[]{:S(2)}) async-start(), calls=%async_computation.3 | async-start | bytes 3244032 | tf_op jit(solution)/shard_map/all_gather | solution.py:71
  385.4 514.8 %all-reduce.17.cloned.1.call-start = ((), (), s32[]{:S(2)}) async-start(), calls=%async_computation.4 | async-start | bytes 589824 | tf_op jit(solution)/shard_map/psum | solution.py:59
  452.8 15.0 collective-permute-start.2
  456.2 11.9 collective-permute-start.3
  620.9 13.4 collective-permute-start.4
  625.4 9.0 collective-permute-start.5
  627.0 192.5 %copy-start.37 = (pred[3]{0:T(512)(128)(4,1)}, pred[3]{0:T(512)(128)(4,1)S(1)}, u32[]{:S(2)}) copy-start(pred[3]{0:T(512)(128)(4,1)S(1)} %get-tuple-element.458) | copy-start | bytes 13
  627.0 192.5 %copy-start.39 = (pred[3]{0:T(512)(128)(4,1)}, pred[3]{0:T(512)(128)(4,1)S(1)}, u32[]{:S(2)}) copy-start(pred[3]{0:T(512)(128)(4,1)S(1)} %get-tuple-element.462) | copy-start | bytes 13
  627.0 192.5 %copy-start.41 = (pred[3]{0:T(512)(128)(4,1)}, pred[3]{0:T(512)(128)(4,1)S(1)}, u32[]{:S(2)}) copy-start(pred[3]{0:T(512)(128)(4,1)S(1)} %get-tuple-element.463) | copy-start | bytes 13
  627.0 194.2 %copy-start.29 = (pred[3]{0:T(512)(128)(4,1)}, pred[3]{0:T(512)(128)(4,1)S(1)}, u32[]{:S(2)}) copy-start(pred[3]{0:T(512)(128)(4,1)S(1)} %get-tuple-element.456) | copy-start | bytes 13
  627.0 194.2 %copy-start.31 = (pred[3]{0:T(512)(128)(4,1)}, pred[3]{0:T(512)(128)(4,1)S(1)}, u32[]{:S(2)}) copy-start(pred[3]{0:T(512)(128)(4,1)S(1)} %get-tuple-element.457) | copy-start | bytes 13
  627.0 194.2 %copy-start.33 = (pred[3]{0:T(512)(128)(4,1)}, pred[3]{0:T(512)(128)(4,1)S(1)}, u32[]{:S(2)}) copy-start(pred[3]{0:T(512)(128)(4,1)S(1)} %get-tuple-element.460) | copy-start | bytes 13
  627.0 194.2 %copy-start.35 = (pred[3]{0:T(512)(128)(4,1)}, pred[3]{0:T(512)(128)(4,1)S(1)}, u32[]{:S(2)}) copy-start(pred[3]{0:T(512)(128)(4,1)S(1)} %get-tuple-element.461) | copy-start | bytes 13
  627.0 196.3 %copy-start.27 = (pred[3]{0:T(512)(128)(4,1)}, pred[3]{0:T(512)(128)(4,1)S(1)}, u32[]{:S(2)}) copy-start(pred[3]{0:T(512)(128)(4,1)S(1)} %get-tuple-element.459) | copy-start | bytes 13
  826.5 137.1 %all-gather.9.cloned.1.call-start = ((), (), s32[]{:S(2)}) async-start(), calls=%async_computation.5 | async-start | bytes 3244032 | tf_op jit(solution)/shard_map/all_gather | solution.py:71
  902.1 583.2 %all-reduce.21.cloned.1.call-start = ((), (), s32[]{:S(2)}) async-start(), calls=%async_computation.8 | async-start | bytes 884736 | tf_op jit(solution)/shard_map/psum | solution.py:220
  1216.5 75.5 %collective-permute-start.6 = (bf16[3,48,1,258]{3,1,2,0:T(8,128)(2,1)}, bf16[3,48,1,258]{3,1,2,0:T(8,128)(2,1)}, u32[]{:S(2)}, u32[]{:S(2)}) collective-permute-start(bf16[3,48,1,258]{3,1,2,0:T(8,128)(2,1)} %copy.2824), channel_id=1, source_target_pairs={{0,1},{1,2},{2,3},{3,4},{4,5},{5,6},{6,7},{8,9},{9,10},{10,11},{11... | collective-permute-start | bytes 222920 | tf_op jit(solution)/shard_map/ppermute | solution.py:19
  1231.5 60.5 %collective-permute-start.7 = (bf16[3,48,1,258]{3,1,2,0:T(8,128)(2,1)}, bf16[3,48,1,258]{3,1,2,0:T(8,128)(2,1)}, u32[]{:S(2)}, u32[]{:S(2)}) collective-permute-start(bf16[3,48,1,258]{3,1,2,0:T(8,128)(2,1)} %copy.2825), channel_id=1, source_target_pairs={{1,0},{2,1},{3,2},{4,3},{5,4},{6,5},{7,6},{9,8},{10,9},{11,10},{12... | collective-permute-start | bytes 222920 | tf_op jit(solution)/shard_map/ppermute | solution.py:22
  1290.2 268.2 %all-reduce.19.cloned.1.call-start = ((), (), s32[]{:S(2)}) async-start(), calls=%async_computation.6 | async-start | bytes 589824 | tf_op jit(solution)/shard_map/psum | solution.py:59
  1485.2 135.7 %all-reduce.23.cloned.1.call-start = ((), (), s32[]{:S(2)}) async-start(), calls=%async_computation.9 | async-start | bytes 884736 | tf_op jit(solution)/shard_map/psum | solution.py:219
  1485.9 169.8 %all-gather.11.cloned.1.call-start = ((), (), s32[]{:S(2)}) async-start(), calls=%async_computation.7 | async-start | bytes 3244032 | tf_op jit(solution)/shard_map/all_gather | solution.py:71
  (39 other events, 970.8 us)
Sparse Core Ops, SparseCore 0:
  19.3 74.3 all-reduce.12
  97.6 58.2 all-gather.4
  311.5 72.1 all-reduce.14
  387.0 58.1 all-gather.6
  826.7 73.5 all-reduce.16
  904.0 58.1 all-gather.8
  1290.3 73.4 all-reduce.20
  1485.3 73.0 all-reduce.18
  1561.1 31.8 all-reduce.22
  1596.2 59.4 all-gather.10
